TPU v7x, 32 devices: a whole 2x2x4 slice. The times are simulated.
32 devices in a mesh: dp: 8 (over z, y), mp: 4 (over x, core).
Axes of the slice: x: 2, y: 2, z: 4, core: 2. Of those that a mesh axis runs over, the one named last changes fastest.
Arguments:
- hidden: bfloat16 [16, 64, 3584], P('dp', None, 'mp'), may hold values from -6 to 6
- rewards: float32 [16, 64], P('dp'), may hold values from -6 to 6
- actions: int32 [16, 64], P('dp'), may hold values from 0 to 152063, as said below
- lengths: int32 [16], P('dp'), may hold values from 1 to 64, 512 in all
- table: bfloat16 [152064, 3584], P('dp', 'mp'), may hold values from -0.09375 to 0.09375
- q_one: bfloat16 [3584, 3584], P('dp', 'mp'), may hold values from -0.09375 to 0.09375
- q_two: bfloat16 [3584, 3584], P('dp', 'mp'), may hold values from -0.09375 to 0.09375
- t_one: bfloat16 [3584, 3584], P('dp', 'mp'), may hold values from -0.09375 to 0.09375
- t_two: bfloat16 [3584, 3584], P('dp', 'mp'), may hold values from -0.09375 to 0.09375
- value_weight: bfloat16 [3584], P('mp'), may hold values from -0.09375 to 0.09375
- value_bias: float32 [1], replicated, may hold values from -3 to 3
Outputs:
- loss: float32 [], replicated
- grad_q_one: float32 [3584, 3584], P('dp', 'mp')
- grad_q_two: float32 [3584, 3584], P('dp', 'mp')
- grad_value: float32 [3584], P('mp')
- grad_bias: float32 [1], replicated
- target_one: bfloat16 [3584, 3584], P('dp', 'mp')
- target_two: bfloat16 [3584, 3584], P('dp', 'mp')
Inputs may be any that keep to these rules, and one draw needn't show every extreme that they name: `actions`: among the 128 positions of the prompts of one index of dp, exactly 16 action ids fall in each of the aligned blocks of 19008 vocabulary rows.
All inputs are finite; a program needn't handle non-finite values. No bound on the sum of `lengths` on one device may be relied on, other than what follows from the above.
Results may differ from a plain program's by a relative error of at most 0.0045.
Values may be sent and summed in bfloat16 or wider, within the bound.
A program may use at most 192 MiB of HBM per device.

v0:
```python
import jax
import jax.numpy as jnp
from jax import lax
from jax.sharding import PartitionSpec as P

discount = 0.99
expectile = 0.7
polyak_rate = 0.005
f32 = jnp.float32
bf16 = jnp.bfloat16


def head_gelu(inputs):
    return jax.nn.gelu(inputs, approximate=True)


def slope(preact, upstream):
    _, pullback = jax.vjp(head_gelu, preact)
    return pullback(upstream)[0]


def pick(mask, row):
    return jnp.sum(jnp.where(mask, row[None, :], jnp.zeros((), row.dtype)), axis=1)


def on_device(
    hidden, rewards, actions, lengths, table, q_one, q_two, t_one, t_two, value_weight, value_bias
):
    dp = lax.axis_size("dp")
    me = lax.axis_index("dp")
    prompts, slots, width = hidden.shape
    own = prompts * slots
    total = own * dp
    packed = total // 2
    share = packed // dp
    cols = q_one.shape[1]
    rows = q_one.shape[0]
    local_rows = table.shape[0]
    local_flat = hidden.reshape(own, width)
    stacked = jnp.concatenate([local_flat, value_weight.reshape(1, width)], axis=0)
    wide = lax.all_gather(stacked, "mp", axis=1, tiled=True)
    flat, value_row = (wide[:own], wide[own:])
    values = (
        jnp.sum(flat.astype(f32) * value_row.astype(f32), axis=1).reshape(prompts, slots)
        + value_bias[0]
    )
    positions = jnp.arange(slots, dtype=jnp.int32)[None, :]
    follows = positions + 1 < lengths[:, None]
    shifted = jnp.concatenate([values[:, 1:], jnp.zeros_like(values[:, :1])], axis=1)
    target = rewards + discount * jnp.where(follows, shifted, 0.0)
    ints = jnp.concatenate([actions, lengths[:, None]], axis=1)
    all_ints = lax.all_gather(ints, "dp", axis=0, tiled=True)
    all_lengths = all_ints[:, slots]
    ids = all_ints[:, :slots].reshape(total)
    facts = jnp.stack([target.reshape(own), values.reshape(own)])
    all_facts = lax.all_gather(facts, "dp", axis=1, tiled=True)
    count = jnp.sum(all_lengths).astype(f32)
    factor = 1.0 / count
    prompt_ids = jnp.arange(prompts * dp, dtype=jnp.int32)
    offsets = jnp.sum(
        jnp.where(prompt_ids[None, :] < prompt_ids[:, None], all_lengths[None, :], 0), axis=1
    )
    place = jnp.where(positions < all_lengths[:, None], offsets[:, None] + positions, -1).reshape(
        total
    )
    own_slots = jnp.arange(share, dtype=jnp.int32)[:, None] + me * share
    own_mask = own_slots == place[None, :]
    holders = ids // local_rows
    by_source = holders.reshape(dp, own)
    order = jnp.arange(own, dtype=jnp.int32)
    earlier = (by_source[:, :, None] == by_source[:, None, :]) & (
        order[None, None, :] < order[None, :, None]
    )
    per_source = own // dp
    rank = (
        jnp.sum(earlier.astype(jnp.int32), axis=2)
        + jnp.arange(dp, dtype=jnp.int32)[:, None] * per_source
    ).reshape(total)
    where_held = holders * own + rank
    wanted = jnp.arange(own, dtype=jnp.int32)[:, None] + me * own == where_held[None, :]
    requests = pick(wanted, ids - me * local_rows)
    found = table[requests]
    all_found = lax.all_gather(found, "dp", axis=0, tiled=True)
    seat = pick(own_mask, where_held)
    seat_mask = (jnp.arange(total, dtype=jnp.int32)[None, :] == seat[:, None]).astype(bf16)
    embed = jnp.dot(seat_mask, all_found, preferred_element_type=f32)
    spread = lax.all_to_all(flat, "dp", split_axis=1, concat_axis=0, tiled=True)
    pack_mask = (jnp.arange(packed, dtype=jnp.int32)[:, None] == place[None, :]).astype(bf16)
    held = jnp.dot(pack_mask, spread, preferred_element_type=f32).astype(bf16)
    partial = jnp.concatenate(
        [
            jnp.dot(held, weight, preferred_element_type=f32).astype(bf16)
            for weight in (q_one, q_two, t_one, t_two)
        ],
        axis=1,
    )
    swapped = lax.all_to_all(partial, "dp", split_axis=0, concat_axis=0, tiled=True)
    pre = jnp.sum(swapped.reshape(dp, share, 4 * cols).astype(f32), axis=0)
    pres = [pre[:, k * cols : (k + 1) * cols] for k in range(4)]
    scores = jnp.stack([jnp.sum(head_gelu(p) * embed, axis=1) for p in pres])
    board = lax.dynamic_update_slice(
        jnp.zeros((4, packed), f32), scores, (jnp.zeros((), jnp.int32), me * share)
    )
    all_scores = lax.psum(board, ("dp", "mp"))
    pack_bool = jnp.arange(packed, dtype=jnp.int32)[:, None] == place[None, :]
    goal = pick(pack_bool, all_facts[0])
    worth = pick(pack_bool, all_facts[1])
    lowest = jnp.minimum(all_scores[2], all_scores[3])
    spread_to = lowest - worth
    weights = jnp.where(spread_to < 0.0, 1.0 - expectile, expectile)
    err_one = all_scores[0] - goal
    err_two = all_scores[1] - goal
    loss = jnp.sum(err_one * err_one + err_two * err_two + weights * spread_to * spread_to) * factor
    grad_values = -2.0 * weights * spread_to
    bias_grad = jnp.sum(grad_values) * factor
    up_one = lax.dynamic_slice(2.0 * err_one, (me * share,), (share,))
    up_two = lax.dynamic_slice(2.0 * err_two, (me * share,), (share,))
    back = jnp.concatenate(
        [
            slope(pres[0], up_one[:, None] * embed).astype(bf16),
            slope(pres[1], up_two[:, None] * embed).astype(bf16),
        ],
        axis=1,
    )
    all_back = lax.all_gather(back, "dp", axis=0, tiled=True)
    dims = (((0,), (0,)), ((), ()))
    head_one = lax.dot_general(held, all_back[:, :cols], dims, preferred_element_type=f32) * factor
    head_two = lax.dot_general(held, all_back[:, cols:], dims, preferred_element_type=f32) * factor
    own_place = lax.dynamic_slice(place, (me * own,), (own,))
    own_errors = pick(
        own_place[:, None] == jnp.arange(packed, dtype=jnp.int32)[None, :], grad_values
    )
    value_part = jnp.sum(own_errors[:, None] * local_flat.astype(f32), axis=0)
    value_grad = lax.psum(value_part * factor, "dp")
    new_one = ((1.0 - polyak_rate) * t_one.astype(f32) + polyak_rate * q_one.astype(f32)).astype(
        bf16
    )
    new_two = ((1.0 - polyak_rate) * t_two.astype(f32) + polyak_rate * q_two.astype(f32)).astype(
        bf16
    )
    return (loss, head_one, head_two, value_grad, bias_grad.reshape(1), new_one, new_two)


def solution(mesh):
    in_specs = (
        P("dp", None, "mp"),
        P("dp", None),
        P("dp", None),
        P("dp"),
        P("dp", "mp"),
        P("dp", "mp"),
        P("dp", "mp"),
        P("dp", "mp"),
        P("dp", "mp"),
        P("mp"),
        P(),
    )
    out_specs = (P(), P("dp", "mp"), P("dp", "mp"), P("mp"), P(), P("dp", "mp"), P("dp", "mp"))
    return jax.shard_map(
        on_device, mesh=mesh, in_specs=in_specs, out_specs=out_specs, check_vma=False
    )
```

profile of v0, /device:TPU:0, one launch (start us, length us, event | category | flops | bytes accessed | tf_op | source)
XLA Modules:
  0.0 288.4 jit_solution(14997182306145007077)
XLA Ops:
  7.2 0.7 reshape.239
  7.9 1.0 pad_maximum_fusion.1
  8.8 11.1 %all_gather.16 = bf16[129,3584]{1,0:T(8,128)(2,1)S(1)} all-gather(bf16[129,896]{1,0:T(8,128)(2,1)S(1)} %pad_maximum_fusion.1), channel_id=1, replica_groups=mesh['dp'=8,'mp'=4] {'mp'}, dimensions={1}, use_global_device_ids=true | all-gather | bytes 1155840 | tf_op jit(solution)/shard_map/all_gather | solution.py:41
  19.9 0.1 slice.71
  20.0 1.3 copy.34
  21.3 5.8 %all-to-all-start = ((bf16[128,8,448]{0,2,1:T(8,128)(2,1)}), bf16[128,8,448]{0,2,1:T(8,128)(2,1)S(1)}, u32[]{:S(2)}, u32[]{:S(2)}) async-start(bf16[128,8,448]{0,2,1:T(8,128)(2,1)} %bitcast.5), calls=%async_computation | async-start | bytes 1835008 | tf_op jit(solution)/shard_map/all_to_all | solution.py:87
  27.1 0.1 copy.32
  27.2 0.1 add_bitcast_fusion
  27.3 30.6 %all-gather.1 = s32[8,2,65]{2,1,0:T(2,128)S(1)} all-gather(s32[1,2,65]{2,1,0:T(2,128)S(1)} %add_bitcast_fusion), channel_id=1, replica_groups=mesh['dp'=8,'mp'=4] {'dp'}, dimensions={0}, use_global_device_ids=true | all-gather | bytes 4680 | tf_op jit(solution)/shard_map/all_gather | solution.py:52
  57.9 0.7 slice_reduce_fusion
  58.6 0.1 copy.36
  58.6 0.1 select_reduce_fusion.5
  58.8 0.1 add_select_fusion
  58.8 0.1 select_n.85
  58.9 0.7 fusion.1
  59.6 0.7 convolution_convert_fusion
  60.4 0.4 copy-done.3
  60.8 0.7 convolution_convert_fusion.1
  61.5 0.4 copy-done.4
  61.9 0.7 convolution_convert_fusion.2
  62.6 0.4 copy-done.5
  63.1 0.7 convolution_convert_fusion.3
  63.8 2.0 pad_maximum_fusion
  65.8 4.5 %all-to-all-start.1 = ((bf16[8,64,3584]{2,1,0:T(8,128)(2,1)}), bf16[8,64,3584]{2,1,0:T(8,128)(2,1)}, u32[]{:S(2)}, u32[]{:S(2)}) async-start(bf16[8,64,3584]{2,1,0:T(8,128)(2,1)} %bitcast.50), calls=%async_computation.1 | async-start | bytes 7340032 | tf_op jit(solution)/shard_map/all_to_all | solution.py:97
  70.3 0.0 all-gather.7.cloned.1.call-start
  70.4 0.1 and.32
  70.5 0.1 and.33
  70.6 0.1 div.28
  70.6 0.1 div.29
  70.7 0.1 sub.43
  70.8 0.4 convert_reduce_fusion.1
  71.2 0.1 fusion.44
  71.3 0.2 select_reduce_fusion.2
  71.5 2.9 %gather_fusion = bf16[128,896]{1,0:T(8,128)(2,1)} fusion(bf16[19008,896]{1,0:T(8,128)(2,1)} %param.15, s32[1024]{0:T(1024)S(1)} %pad_clamp_fusion), kind=kCustom, calls=%fused_computation | custom fusion | bytes 459264 | tf_op jit(solution)/shard_map/gather | solution.py:82
  74.4 0.0 all-gather.7.cloned.1.call-update
  74.4 0.0 all-gather.5.cloned.1.call-start
  75.2 0.3 multiply_reduce_fusion
  75.5 0.1 add.202
  75.5 0.1 slice.60
  75.6 0.1 fusion.52
  75.7 0.1 stack_reshape.4
  75.8 83.3 %all_gather.18 = f32[2,1024]{1,0:T(2,128)S(1)} all-gather(f32[2,128]{1,0:T(2,128)S(1)} %pad_maximum_fusion.4), channel_id=1, replica_groups=mesh['dp'=8,'mp'=4] {'dp'}, dimensions={1}, use_global_device_ids=true | all-gather | bytes 9216 | tf_op jit(solution)/shard_map/all_gather | solution.py:56
  159.1 0.2 select_reduce_fusion.4
  159.3 0.7 select_reduce_fusion.1
  160.0 12.1 %all-to-all-done.1 = bf16[8,64,3584]{2,1,0:T(8,128)(2,1)} async-done(((bf16[8,64,3584]{2,1,0:T(8,128)(2,1)}), bf16[8,64,3584]{2,1,0:T(8,128)(2,1)}, u32[]{:S(2)}, u32[]{:S(2)}) %all-to-all-start.1) | async-done | bytes 3670048 | tf_op jit(solution)/shard_map/all_to_all | solution.py:97
  172.1 2.6 convert_reduce_fusion
  174.7 0.0 all-gather.7.cloned.1.call-done
  174.7 2.3 multiply_reduce_fusion.3
  177.0 0.2 dynamic_update_slice.3
  177.2 48.2 %psum.14 = f32[4,512]{1,0:T(4,128)S(1)} all-reduce(f32[4,512]{1,0:T(4,128)S(1)} %dynamic_update_slice.3), channel_id=1, replica_groups=mesh['dp'=8,'mp'=4] {'dp','mp'}, use_global_device_ids=true, to_apply=%region_9.10 | all-reduce | flops 2048 | bytes 16384 | tf_op jit(solution)/shard_map/psum | solution.py:104
  225.5 0.6 fusion.46
  226.1 0.1 dynamic_slice.9
  226.2 0.1 dynamic_slice.10
  226.2 0.3 fusion.14
  226.6 0.7 pad_maximum_fusion.2
  227.9 0.1 dynamic_slice.11
  228.1 3.2 %add_convert_fusion = (bf16[448,896]{1,0:T(8,128)(2,1)}, bf16[448,896]{1,0:T(8,128)(2,1)}) fusion(bf16[448,896]{1,0:T(8,128)(2,1)} %param.17, bf16[448,896]{1,0:T(8,128)(2,1)S(1)} %copy-done.2, bf16[448,896]{1,0:T(8,128)(2,1)} %param.16, bf16[448,896]{1,0:T(8,128)(2,1)S(1)} %copy-done.3), kind=kLoop, calls=%fused_computation.8 | loop fusion | flops 4816896 | bytes 4816896 | tf_op jit(solution)/shard_map/convert_element_type | solution.py:138
  231.3 0.2 select_reduce_fusion.3
  231.5 0.1 mul.336
  232.9 0.1 multiply_reduce_fusion.1
  233.0 21.8 %psum.15 = f32[896]{0:T(1024)} all-reduce(f32[896]{0:T(1024)S(1)} %broadcast_multiply_fusion), channel_id=1, replica_groups=mesh['dp'=8,'mp'=4] {'dp'}, use_global_device_ids=true, to_apply=%region_17.18 | all-reduce | flops 896 | bytes 7168 | tf_op jit(solution)/shard_map/psum | solution.py:134
  254.8 19.6 %all-gather.5.cloned.1.call-done = bf16[512,1792]{1,0:T(8,128)(2,1)} async-done(((bf16[64,1792]{1,0:T(8,128)(2,1)}), bf16[512,1792]{1,0:T(8,128)(2,1)}) %all-gather.5.cloned.1.call-update) | async-done | bytes 1835024 | tf_op jit(solution)/shard_map/all_gather | solution.py:125
  274.4 3.1 %convolution_multiply_fusion.1 = f32[448,896]{1,0:T(8,128)} fusion(bf16[512,448]{0,1:T(8,128)(2,1)S(1)} %fusion.1, bf16[512,1792]{1,0:T(8,128)(2,1)} %all-gather.5.cloned.1.call-done, f32[]{:T(128)S(6)} %div.30), kind=kOutput, calls=%fused_computation.11 | convolution fusion | flops 411443200 | bytes 2981892 | tf_op jit(solution)/shard_map/dot_general | solution.py:127
  277.5 1.8 convolution_multiply_fusion
  (36 shorter events, 0.2 us)
Async XLA Ops:
  20.0 7.1 %copy-start.8 = (s32[2]{0:T(128)S(1)}, s32[2]{0:T(128)}, u32[]{:S(2)}) copy-start(s32[2]{0:T(128)} %param.14) | copy-start | bytes 28
  20.0 7.2 %copy-start.6 = (s32[2,64]{1,0:T(2,128)S(1)}, s32[2,64]{1,0:T(2,128)}, u32[]{:S(2)}) copy-start(s32[2,64]{1,0:T(2,128)} %param.13) | copy-start | bytes 1540
  21.3 37.6 %all-to-all-start = ((bf16[128,8,448]{0,2,1:T(8,128)(2,1)}), bf16[128,8,448]{0,2,1:T(8,128)(2,1)S(1)}, u32[]{:S(2)}, u32[]{:S(2)}) async-start(bf16[128,8,448]{0,2,1:T(8,128)(2,1)} %bitcast.5), calls=%async_computation | async-start | bytes 1835008 | tf_op jit(solution)/shard_map/all_to_all | solution.py:87
  27.1 32.5 %copy-start.2 = (bf16[448,896]{1,0:T(8,128)(2,1)S(1)}, bf16[448,896]{1,0:T(8,128)(2,1)}, u32[]{:S(2)}) copy-start(bf16[448,896]{1,0:T(8,128)(2,1)} %param.19) | copy-start | bytes 2408452
  59.6 1.1 copy-start.3
  60.8 1.1 copy-start.4
  61.9 1.1 copy-start.5
  65.8 106.3 %all-to-all-start.1 = ((bf16[8,64,3584]{2,1,0:T(8,128)(2,1)}), bf16[8,64,3584]{2,1,0:T(8,128)(2,1)}, u32[]{:S(2)}, u32[]{:S(2)}) async-start(bf16[8,64,3584]{2,1,0:T(8,128)(2,1)} %bitcast.50), calls=%async_computation.1 | async-start | bytes 7340032 | tf_op jit(solution)/shard_map/all_to_all | solution.py:97
  70.3 5.3 %copy-start.7 = (f32[2,64]{1,0:T(2,128)S(1)}, f32[2,64]{1,0:T(2,128)}, u32[]{:S(2)}) copy-start(f32[2,64]{1,0:T(2,128)} %param.12) | copy-start | bytes 1540
  70.3 104.4 %all-gather.7.cloned.1.call-start = ((), (), s32[]{:S(2)}) async-start(), calls=%async_computation.3 | async-start | bytes 2064384 | tf_op jit(solution)/shard_map/all_gather | solution.py:83
  74.4 199.9 %all-gather.5.cloned.1.call-start = ((), (), s32[]{:S(2)}) async-start(), calls=%async_computation.2 | async-start | bytes 2064384 | tf_op jit(solution)/shard_map/all_gather | solution.py:125
  228.1 4.8 %copy-start.1 = (bf16[2,64,896]{2,1,0:T(8,128)(2,1)S(1)}, bf16[2,64,896]{2,1,0:T(8,128)(2,1)}, u32[]{:S(2)}) copy-start(bf16[2,64,896]{2,1,0:T(8,128)(2,1)} %param.11) | copy-start | bytes 688132
  274.4 3.1 %copy-start = (bf16[512,1792]{1,0:T(8,128)(2,1)S(1)}, bf16[512,1792]{1,0:T(8,128)(2,1)}, u32[]{:S(2)}) copy-start(bf16[512,1792]{1,0:T(8,128)(2,1)} %all-gather.5.cloned.1.call-done) | copy-start | bytes 5505028
Sparse Core Ops, SparseCore 0:
  74.5 86.5 all-gather.6
  227.4 46.9 all-gather.4
where the time goes:
time: 289 us; the launch traced here: 288 us
  blocking collectives  195 us (67%)
  waiting for transfers between devices  31.8 us (11%)
  between operations  19.2 us (7%)
  other arithmetic  13.7 us (5%)
  matrix products  10.8 us (4%)
  starting transfers between devices  10.4 us (4%)
  local copies, waits for them, and re-layouts  7.53 us (3%)
    all_gather x1, blocking collectives, on_device(): all_facts = lax.all_gather(facts, 'dp', axis=1, tiled=True)  83.3 us
    psum x1, blocking collectives, on_device(): all_scores = lax.psum(board, ('dp', 'mp'))  48.2 us
    all_gather x1, blocking collectives, on_device(): all_ints = lax.all_gather(ints, 'dp', axis=0, tiled=True)  30.6 us
    psum x1, blocking collectives, on_device(): value_grad = lax.psum(value_part * factor, 'dp')  21.8 us
    all_gather x1, waiting for transfers between devices, on_device(): all_back = lax.all_gather(back, 'dp', axis=0, tiled=True)  19.6 us
    all_to_all x1, waiting for transfers between devices, on_device(): lax.all_to_all(partial, 'dp', split_axis=0, concat_axis=0, tiled=True)  12.1 us
    all_gather x1, blocking collectives, on_device(): wide = lax.all_gather(stacked, 'mp', axis=1, tiled=True)  11.1 us
    all_to_all x1, starting transfers between devices, on_device(): spread = lax.all_to_all(flat, 'dp', split_axis=1, concat_axis=0, tiled=True)  5.83 us
  transfers between devices with their start and end apart: 4, of which 2 were waited for; matrix products, arithmetic and copies ran while one was open for 5% of the time, Pallas kernels for 0%

commit v1 on v0

--- a/solution.py
+++ b/solution.py
@@ -101,7 +101,7 @@
     board = lax.dynamic_update_slice(
         jnp.zeros((4, packed), f32), scores, (jnp.zeros((), jnp.int32), me * share)
     )
-    all_scores = lax.psum(board, ("dp", "mp"))
+    all_scores = jnp.sum(lax.all_gather(board, ("dp", "mp")), axis=0)
     pack_bool = jnp.arange(packed, dtype=jnp.int32)[:, None] == place[None, :]
     goal = pick(pack_bool, all_facts[0])
     worth = pick(pack_bool, all_facts[1])

time: 289 us -> 286 us (0.990)
  blocking collectives: 195 us -> 192 us
    all_gather x0 -> x1, blocking collectives: none -> 48.9 us  [on_device(): all_scores = jnp.sum(lax.all_gather(board, ('dp', 'mp')), axis=0)]
    psum x1 -> x0, blocking collectives: 48.2 us -> none  [on_device(): all_scores = lax.psum(board, ('dp', 'mp'))]
    psum x1, blocking collectives: 21.8 us -> 17.8 us  [on_device(): value_grad = lax.psum(value_part * factor, 'dp')]
where the time goes in v1:
time: 286 us; the launch traced here: 285 us
  blocking collectives  192 us (67%)
  waiting for transfers between devices  31.6 us (11%)
  between operations  19.2 us (7%)
  other arithmetic  13.8 us (5%)
  matrix products  10.8 us (4%)
  starting transfers between devices  10.4 us (4%)
  local copies, waits for them, and re-layouts  7.53 us (3%)
    all_gather x1, blocking collectives, on_device(): all_facts = lax.all_gather(facts, 'dp', axis=1, tiled=True)  83.3 us
    all_gather x1, blocking collectives, on_device(): all_scores = jnp.sum(lax.all_gather(board, ('dp', 'mp')), axis=0)  48.9 us
    all_gather x1, blocking collectives, on_device(): all_ints = lax.all_gather(ints, 'dp', axis=0, tiled=True)  30.6 us
    all_gather x1, waiting for transfers between devices, on_device(): all_back = lax.all_gather(back, 'dp', axis=0, tiled=True)  19.4 us
    psum x1, blocking collectives, on_device(): value_grad = lax.psum(value_part * factor, 'dp')  17.8 us
    all_to_all x1, waiting for transfers between devices, on_device(): lax.all_to_all(partial, 'dp', split_axis=0, concat_axis=0, tiled=True)  12.1 us
    all_gather x1, blocking collectives, on_device(): wide = lax.all_gather(stacked, 'mp', axis=1, tiled=True)  11.1 us
    all_to_all x1, starting transfers between devices, on_device(): spread = lax.all_to_all(flat, 'dp', split_axis=1, concat_axis=0, tiled=True)  5.83 us
  transfers between devices with their start and end apart: 4, of which 2 were waited for; matrix products, arithmetic and copies ran while one was open for 5% of the time, Pallas kernels for 0%

profile of v1, /device:TPU:0, one launch (start us, length us, event | category | flops | bytes accessed | tf_op | source)
XLA Modules:
  0.0 284.9 jit_solution(13683743620185590132)
XLA Ops:
  7.2 0.7 reshape.241
  7.9 1.0 pad_maximum_fusion.1
  8.8 11.1 %all_gather.22 = bf16[129,3584]{1,0:T(8,128)(2,1)S(1)} all-gather(bf16[129,896]{1,0:T(8,128)(2,1)S(1)} %pad_maximum_fusion.1), channel_id=1, replica_groups=mesh['dp'=8,'mp'=4] {'mp'}, dimensions={1}, use_global_device_ids=true | all-gather | bytes 1155840 | tf_op jit(solution)/shard_map/all_gather | solution.py:41
  19.9 0.1 slice.71
  20.0 1.3 copy.34
  21.3 5.8 %all-to-all-start = ((bf16[128,8,448]{0,2,1:T(8,128)(2,1)}), bf16[128,8,448]{0,2,1:T(8,128)(2,1)S(1)}, u32[]{:S(2)}, u32[]{:S(2)}) async-start(bf16[128,8,448]{0,2,1:T(8,128)(2,1)} %bitcast.5), calls=%async_computation | async-start | bytes 1835008 | tf_op jit(solution)/shard_map/all_to_all | solution.py:87
  27.1 0.1 copy.32
  27.2 0.1 add_bitcast_fusion
  27.3 30.6 %all-gather.1 = s32[8,2,65]{2,1,0:T(2,128)S(1)} all-gather(s32[1,2,65]{2,1,0:T(2,128)S(1)} %add_bitcast_fusion), channel_id=1, replica_groups=mesh['dp'=8,'mp'=4] {'dp'}, dimensions={0}, use_global_device_ids=true | all-gather | bytes 4680 | tf_op jit(solution)/shard_map/all_gather | solution.py:52
  57.9 0.7 slice_reduce_fusion
  58.6 0.1 copy.36
  58.6 0.1 select_reduce_fusion.5
  58.8 0.1 add_select_fusion
  58.8 0.1 select_n.85
  58.9 0.7 fusion.1
  59.6 0.7 convolution_convert_fusion
  60.4 0.4 copy-done.3
  60.8 0.7 convolution_convert_fusion.1
  61.5 0.4 copy-done.4
  61.9 0.7 convolution_convert_fusion.2
  62.6 0.4 copy-done.5
  63.1 0.7 convolution_convert_fusion.3
  63.8 2.0 pad_maximum_fusion
  65.8 4.5 %all-to-all-start.1 = ((bf16[8,64,3584]{2,1,0:T(8,128)(2,1)}), bf16[8,64,3584]{2,1,0:T(8,128)(2,1)}, u32[]{:S(2)}, u32[]{:S(2)}) async-start(bf16[8,64,3584]{2,1,0:T(8,128)(2,1)} %bitcast.52), calls=%async_computation.1 | async-start | bytes 7340032 | tf_op jit(solution)/shard_map/all_to_all | solution.py:97
  70.3 0.0 all-gather.7.cloned.1.call-start
  70.4 0.1 and.32
  70.5 0.1 and.33
  70.6 0.1 div.28
  70.6 0.1 div.29
  70.7 0.1 sub.43
  70.8 0.4 convert_reduce_fusion.1
  71.2 0.1 fusion.44
  71.3 0.2 select_reduce_fusion.2
  71.5 2.9 %gather_fusion = bf16[128,896]{1,0:T(8,128)(2,1)} fusion(bf16[19008,896]{1,0:T(8,128)(2,1)} %param.15, s32[1024]{0:T(1024)S(1)} %pad_clamp_fusion), kind=kCustom, calls=%fused_computation | custom fusion | bytes 459264 | tf_op jit(solution)/shard_map/gather | solution.py:82
  74.4 0.0 all-gather.5.cloned.1.call-start
  75.2 0.3 multiply_reduce_fusion
  75.5 0.1 add.200
  75.5 0.1 slice.60
  75.6 0.1 fusion.52
  75.7 0.1 stack_reshape.4
  75.8 83.3 %all_gather.26 = f32[2,1024]{1,0:T(2,128)S(1)} all-gather(f32[2,128]{1,0:T(2,128)S(1)} %pad_maximum_fusion.3), channel_id=1, replica_groups=mesh['dp'=8,'mp'=4] {'dp'}, dimensions={1}, use_global_device_ids=true | all-gather | bytes 9216 | tf_op jit(solution)/shard_map/all_gather | solution.py:56
  159.1 0.2 select_reduce_fusion.4
  159.3 0.7 select_reduce_fusion.1
  160.0 12.1 %all-to-all-done.1 = bf16[8,64,3584]{2,1,0:T(8,128)(2,1)} async-done(((bf16[8,64,3584]{2,1,0:T(8,128)(2,1)}), bf16[8,64,3584]{2,1,0:T(8,128)(2,1)}, u32[]{:S(2)}, u32[]{:S(2)}) %all-to-all-start.1) | async-done | bytes 3670048 | tf_op jit(solution)/shard_map/all_to_all | solution.py:97
  172.1 2.6 convert_reduce_fusion
  174.7 0.0 all-gather.7.cloned.1.call-done
  174.7 2.3 multiply_reduce_fusion.3
  177.0 0.2 dynamic_update_slice.4
  177.2 48.9 %all_gather.25 = f32[32,4,512]{2,1,0:T(4,128)S(1)} all-gather(f32[1,4,512]{2,1,0:T(4,128)S(1)} %dynamic_update_slice.4), channel_id=1, replica_groups=mesh['dp'=8,'mp'=4] {'dp','mp'}, dimensions={0}, use_global_device_ids=true | all-gather | bytes 270336 | tf_op jit(solution)/shard_map/all_gather | solution.py:104
  226.1 0.1 reduce_sum.176
  226.2 0.6 fusion.46
  226.8 0.1 dynamic_slice.9
  226.9 0.1 dynamic_slice.10
  226.9 0.3 fusion.14
  227.3 0.7 pad_maximum_fusion.2
  228.6 0.1 dynamic_slice.11
  228.8 3.2 %add_convert_fusion = (bf16[448,896]{1,0:T(8,128)(2,1)}, bf16[448,896]{1,0:T(8,128)(2,1)}) fusion(bf16[448,896]{1,0:T(8,128)(2,1)} %param.17, bf16[448,896]{1,0:T(8,128)(2,1)S(1)} %copy-done.2, bf16[448,896]{1,0:T(8,128)(2,1)} %param.16, bf16[448,896]{1,0:T(8,128)(2,1)S(1)} %copy-done.3), kind=kLoop, calls=%fused_computation.8 | loop fusion | flops 4816896 | bytes 4816896 | tf_op jit(solution)/shard_map/convert_element_type | solution.py:138
  232.0 0.2 select_reduce_fusion.3
  232.2 0.1 mul.336
  233.6 0.1 multiply_reduce_fusion.1
  233.7 17.8 %psum.7 = f32[896]{0:T(1024)} all-reduce(f32[896]{0:T(1024)S(1)} %broadcast_multiply_fusion), channel_id=1, replica_groups=mesh['dp'=8,'mp'=4] {'dp'}, use_global_device_ids=true, to_apply=%region_17.18 | all-reduce | flops 896 | bytes 7168 | tf_op jit(solution)/shard_map/psum | solution.py:134
  251.5 19.4 %all-gather.5.cloned.1.call-done = bf16[512,1792]{1,0:T(8,128)(2,1)} async-done(((bf16[64,1792]{1,0:T(8,128)(2,1)}), bf16[512,1792]{1,0:T(8,128)(2,1)}) %all-gather.5.cloned.1.call-update) | async-done | bytes 1835024 | tf_op jit(solution)/shard_map/all_gather | solution.py:125
  270.9 3.1 %convolution_multiply_fusion.1 = f32[448,896]{1,0:T(8,128)} fusion(bf16[512,448]{0,1:T(8,128)(2,1)S(1)} %fusion.1, bf16[512,1792]{1,0:T(8,128)(2,1)} %all-gather.5.cloned.1.call-done, f32[]{:T(128)S(6)} %div.30), kind=kOutput, calls=%fused_computation.11 | convolution fusion | flops 411443200 | bytes 2981892 | tf_op jit(solution)/shard_map/dot_general | solution.py:127
  274.0 1.8 convolution_multiply_fusion
  (37 shorter events, 0.2 us)
Async XLA Ops:
  20.0 7.1 %copy-start.8 = (s32[2]{0:T(128)S(1)}, s32[2]{0:T(128)}, u32[]{:S(2)}) copy-start(s32[2]{0:T(128)} %param.14) | copy-start | bytes 28
  20.0 7.2 %copy-start.6 = (s32[2,64]{1,0:T(2,128)S(1)}, s32[2,64]{1,0:T(2,128)}, u32[]{:S(2)}) copy-start(s32[2,64]{1,0:T(2,128)} %param.13) | copy-start | bytes 1540
  21.3 37.6 %all-to-all-start = ((bf16[128,8,448]{0,2,1:T(8,128)(2,1)}), bf16[128,8,448]{0,2,1:T(8,128)(2,1)S(1)}, u32[]{:S(2)}, u32[]{:S(2)}) async-start(bf16[128,8,448]{0,2,1:T(8,128)(2,1)} %bitcast.5), calls=%async_computation | async-start | bytes 1835008 | tf_op jit(solution)/shard_map/all_to_all | solution.py:87
  27.1 32.5 %copy-start.2 = (bf16[448,896]{1,0:T(8,128)(2,1)S(1)}, bf16[448,896]{1,0:T(8,128)(2,1)}, u32[]{:S(2)}) copy-start(bf16[448,896]{1,0:T(8,128)(2,1)} %param.19) | copy-start | bytes 2408452
  59.6 1.1 copy-start.3
  60.8 1.1 copy-start.4
  61.9 1.1 copy-start.5
  65.8 106.3 %all-to-all-start.1 = ((bf16[8,64,3584]{2,1,0:T(8,128)(2,1)}), bf16[8,64,3584]{2,1,0:T(8,128)(2,1)}, u32[]{:S(2)}, u32[]{:S(2)}) async-start(bf16[8,64,3584]{2,1,0:T(8,128)(2,1)} %bitcast.52), calls=%async_computation.1 | async-start | bytes 7340032 | tf_op jit(solution)/shard_map/all_to_all | solution.py:97
  70.3 5.3 %copy-start.7 = (f32[2,64]{1,0:T(2,128)S(1)}, f32[2,64]{1,0:T(2,128)}, u32[]{:S(2)}) copy-start(f32[2,64]{1,0:T(2,128)} %param.12) | copy-start | bytes 1540
  70.3 104.4 %all-gather.7.cloned.1.call-start = ((), (), s32[]{:S(2)}) async-start(), calls=%async_computation.3 | async-start | bytes 2064384 | tf_op jit(solution)/shard_map/all_gather | solution.py:83
  74.4 196.5 %all-gather.5.cloned.1.call-start = ((), (), s32[]{:S(2)}) async-start(), calls=%async_computation.2 | async-start | bytes 2064384 | tf_op jit(solution)/shard_map/all_gather | solution.py:125
  228.8 4.8 %copy-start.1 = (bf16[2,64,896]{2,1,0:T(8,128)(2,1)S(1)}, bf16[2,64,896]{2,1,0:T(8,128)(2,1)}, u32[]{:S(2)}) copy-start(bf16[2,64,896]{2,1,0:T(8,128)(2,1)} %param.11) | copy-start | bytes 688132
  270.9 3.1 %copy-start = (bf16[512,1792]{1,0:T(8,128)(2,1)S(1)}, bf16[512,1792]{1,0:T(8,128)(2,1)}, u32[]{:S(2)}) copy-start(bf16[512,1792]{1,0:T(8,128)(2,1)} %all-gather.5.cloned.1.call-done) | copy-start | bytes 5505028
Sparse Core Ops, SparseCore 0:
  74.5 86.5 all-gather.6
  228.1 42.7 all-gather.4
